TPU v7x, 256 devices: a whole 4x4x8 slice. The times are simulated.
256 devices in a mesh: samp: 16 (over z_hi, x, core), gene: 4 (over z_lo), snp: 4 (over y).
Axes of the slice: x: 4, y: 4, z: 8 (z_hi: 2, z_lo: 4; z = z_hi * 4 + z_lo), core: 2. Of those that a mesh axis runs over, the one named last changes fastest.
Arguments:
- expression: bfloat16 [4096, 16384], P('samp', ('gene', 'snp')), may hold values from -6 to 6
- loadings: bfloat16 [16384, 128], P(('gene', 'snp')), may hold values from -0.046875 to 0.046875
- dosage: bfloat16 [4096, 16384], P(None, ('gene', 'snp')), may hold values from 0 to 2
Outputs:
- assoc: bfloat16 [16, 16, 64, 16384], P(None, 'samp', None, ('gene', 'snp'))
All inputs are finite; a program needn't handle non-finite values.
Results may differ from a plain program's by a relative error of at most 0.0065.
Values may be sent and summed in bfloat16 or wider, within the bound.
No kernel may reach another device: no remote copies, remote signals or barrier semaphores. Data moves between devices by JAX's collectives and lax.ppermute only.
A program may use at most 64 MiB of HBM per device.

v0:
```python
import jax
import jax.numpy as jnp
from jax import lax
from jax.sharding import PartitionSpec as P

ridge_factor = 1.0
ridge_sample = 1.0


def body(expression, loadings, dosage):
    contract = (((0,), (0,)), ((), ()))
    factor_count = loadings.shape[1]
    identity = jnp.eye(factor_count, dtype=jnp.float32)
    panel_genes = expression.shape[1] // lax.axis_size("samp")
    all_samples = dosage.shape[0]
    snp_count = dosage.shape[1]
    block_count = lax.axis_size("gene") * lax.axis_size("snp")
    norm_scale = 1.0 / jnp.sqrt(jnp.float32(all_samples))
    local_factor = jnp.dot(expression, loadings, preferred_element_type=jnp.float32)
    local_gram = lax.dot_general(loadings, loadings, contract, preferred_element_type=jnp.float32)
    factor_sum, gram_sum = lax.psum((local_factor, local_gram), ("gene", "snp"))
    lower_gram = jnp.linalg.cholesky(gram_sum + ridge_factor * identity)
    factors = jax.scipy.linalg.cho_solve((lower_gram, True), factor_sum.T).T.astype(jnp.bfloat16)
    local_hess = lax.dot_general(factors, factors, contract, preferred_element_type=jnp.float32)
    local_cross = lax.dot_general(factors, expression, contract, preferred_element_type=jnp.float32)
    hess_sum, cross_sum = lax.psum((local_hess, local_cross), "samp")
    lower_hess = jnp.linalg.cholesky(hess_sum + ridge_sample * identity)
    fit_coef = jax.scipy.linalg.cho_solve((lower_hess, True), cross_sum).astype(jnp.bfloat16)
    fitted = lax.dot_general(
        fit_coef, factors, (((0,), (1,)), ((), ())), preferred_element_type=jnp.float32
    )
    residual_t = (expression.T.astype(jnp.float32) - fitted).astype(jnp.bfloat16)
    panel_resid = lax.all_to_all(residual_t, "samp", split_axis=0, concat_axis=1, tiled=True)
    totals = (
        jnp.dot(
            lax.all_gather(panel_resid, ("gene", "snp"), axis=0, tiled=True),
            dosage,
            preferred_element_type=jnp.float32,
        )
        * norm_scale
    )
    return totals.astype(jnp.bfloat16).reshape(block_count, 1, panel_genes, snp_count)


def solution(mesh):
    placed = (P("samp", ("gene", "snp")), P(("gene", "snp"), None), P(None, ("gene", "snp")))
    return jax.shard_map(
        body,
        mesh=mesh,
        in_specs=placed,
        out_specs=P(None, "samp", None, ("gene", "snp")),
        check_vma=False,
    )
```

profile of v0, /device:TPU:1, one launch (start us, length us, event | category | flops | bytes accessed | tf_op | source)
XLA Modules:
  0.0 548.4 jit_solution(741673774838986686)
XLA Ops:
  6.5 0.9 copy-done
  7.5 0.9 fusion.13
  8.4 2.0 fusion.14
  10.4 148.5 %all-reduce.5.cloned.1.call-done = (f32[256,128]{1,0:T(8,128)}, f32[128,128]{0,1:T(8,128)}) async-done(((f32[256,128]{1,0:T(8,128)}, f32[128,128]{0,1:T(8,128)}), (f32[256,128]{1,0:T(8,128)}, f32[128,128]{0,1:T(8,128)})) %all-reduce.5.cloned.1.call-update) | async-done | bytes 196624 | tf_op jit(solution)/shard_map/psum | solution.py:21
  159.0 0.9 convert_add_fusion.1
  159.9 0.9 fusion.10
  160.8 11.7 %cholesky.44 = f32[128,128]{1,0:T(8,128)S(1)} custom-call(f32[128,128]{1,0:T(8,128)S(1)} %fusion.10), custom_call_target="Cholesky" | custom-call | tf_op jit(solution)/shard_map/jit(cholesky)/cholesky | solution.py:22
  173.2 0.7 fusion.1
  173.8 9.8 %custom-call.16 = f32[1,128,128]{1,2,0:T(8,128)S(1)} custom-call(f32[1,128,128]{2,1,0:T(8,128)S(1)} %fusion.1), custom_call_target="InvertDiagBlocksLowerTriangular" | custom-call | tf_op jit(solution)/shard_map/jit(_cho_solve)/triangular_solve | solution.py:23
  183.6 1.2 fusion.8
  185.3 0.8 fusion.15
  186.1 2.1 fusion.16
  188.4 1.2 copy.17
  189.7 183.0 %all-reduce.7.cloned.1.call-done = (f32[128,1024]{1,0:T(8,128)}, f32[128,128]{0,1:T(8,128)}) async-done(((f32[128,1024]{1,0:T(8,128)}, f32[128,128]{0,1:T(8,128)}), (f32[128,1024]{1,0:T(8,128)}, f32[128,128]{0,1:T(8,128)})) %all-reduce.7.cloned.1.call-update) | async-done | bytes 589840 | tf_op jit(solution)/shard_map/psum | solution.py:26
  372.7 0.9 convert_add_fusion
  373.6 0.9 fusion.6
  374.5 11.7 %cholesky.55 = f32[128,128]{1,0:T(8,128)S(1)} custom-call(f32[128,128]{1,0:T(8,128)S(1)} %fusion.6), custom_call_target="Cholesky" | custom-call | tf_op jit(solution)/shard_map/jit(cholesky)/cholesky | solution.py:27
  386.9 0.7 fusion.2
  387.6 9.8 %custom-call.17 = f32[1,128,128]{1,2,0:T(8,128)S(1)} custom-call(f32[1,128,128]{2,1,0:T(8,128)S(1)} %fusion.2), custom_call_target="InvertDiagBlocksLowerTriangular" | custom-call | tf_op jit(solution)/shard_map/jit(_cho_solve)/triangular_solve | solution.py:28
  397.4 1.7 fusion.4
  400.0 21.6 %all_to_all.19 = bf16[16,64,256]{2,1,0:T(8,128)(2,1)S(1)} all-to-all(bf16[16,64,256]{2,1,0:T(8,128)(2,1)S(1)} %bitcast.48), channel_id=1, replica_groups=mesh['samp'=16,'gene'=4,'snp'=4] {'samp'}, dimensions={0} | all-to-all | bytes 1048576 | tf_op jit(solution)/shard_map/all_to_all | solution.py:33
  421.6 0.8 copy.26
  422.5 104.8 %all-gather.2.cloned.1.call-done = bf16[1024,4096]{1,0:T(8,128)(2,1)} async-done(((bf16[64,4096]{1,0:T(8,128)(2,1)}), bf16[1024,4096]{1,0:T(8,128)(2,1)}) %all-gather.2.cloned.1.call-update) | async-done | bytes 8388624 | tf_op jit(solution)/shard_map/all_gather | solution.py:36
  527.3 14.6 %multiply_convert_fusion = bf16[1024,1024]{1,0:T(8,128)(2,1)} fusion(bf16[1024,4096]{1,0:T(8,128)(2,1)} %all-gather.2.cloned.1.call-done, bf16[4096,1024]{1,0:T(8,128)(2,1)} %param.6), kind=kOutput, calls=%fused_computation | convolution fusion | flops 8592031744 | bytes 18874368 | tf_op jit(solution)/shard_map/dot_general | solution.py:35
  (16 shorter events, 3.1 us)
Async XLA Ops:
  6.5 1.0 copy-start
  6.5 152.4 %all-reduce.5.cloned.1.call-start = ((), (), s32[]{:S(2)}) async-start(), calls=%async_computation.2 | async-start | bytes 393216 | tf_op jit(solution)/shard_map/psum | solution.py:21
  10.4 362.3 %all-reduce.7.cloned.1.call-start = ((), (), s32[]{:S(2)}) async-start(), calls=%async_computation.3 | async-start | bytes 1179648 | tf_op jit(solution)/shard_map/psum | solution.py:26
  188.2 339.1 %all-gather.2.cloned.1.call-start = ((), (), s32[]{:S(2)}) async-start(), calls=%async_computation.1 | async-start | bytes 8912896 | tf_op jit(solution)/shard_map/all_gather | solution.py:36
Sparse Core Ops, SparseCore 0:
  10.5 148.4 all-reduce.4
  188.3 184.3 all-reduce.6
  422.6 104.6 all-gather.1
where the time goes:
time: 549 us; the launch traced here: 548 us
  waiting for transfers between devices  436 us (79%)
  other arithmetic  49.1 us (9%)
  matrix products  24.6 us (4%)
  blocking collectives  21.6 us (4%)
  between operations  13.2 us (2%)
    psum x1, waiting for transfers between devices, body(): hess_sum, cross_sum = lax.psum((local_hess, local_cross), 'samp')  183 us
    psum x1, waiting for transfers between devices, body(): factor_sum, gram_sum = lax.psum((local_factor, local_gram), ('gene', 'snp'))  149 us
    all_gather x1, waiting for transfers between devices, body(): lax.all_gather(panel_resid, ('gene', 'snp'), axis=0, tiled=True)  105 us
    all_to_all x1, blocking collectives, body(): lax.all_to_all(residual_t, 'samp', split_axis=0, concat_axis=1, tiled=True)  21.6 us
    dot_general x1, matrix products, body(): jnp.dot(lax.all_gather(panel_resid, ('gene', 'snp'), axis=0, tiled=True),...  14.6 us
    another operation x3, other arithmetic, body(): lower_hess = jnp.linalg.cholesky(hess_sum + ridge_sample * identity)  12.4 us
    another operation x3, other arithmetic, body(): lower_gram = jnp.linalg.cholesky(gram_sum + ridge_factor * identity)  12.4 us
  transfers between devices with their start and end apart: 3, of which 3 were waited for; matrix products, arithmetic and copies ran while one was open for 0% of the time, Pallas kernels for 0%

commit v1 on v0

--- a/solution.py
+++ b/solution.py
@@ -18,7 +18,15 @@
     norm_scale = 1.0 / jnp.sqrt(jnp.float32(all_samples))
     local_factor = jnp.dot(expression, loadings, preferred_element_type=jnp.float32)
     local_gram = lax.dot_general(loadings, loadings, contract, preferred_element_type=jnp.float32)
-    factor_sum, gram_sum = lax.psum((local_factor, local_gram), ("gene", "snp"))
+
+    def sites_lead(row_data):
+        which_axis = "gene"
+        dev_axis = "snp"
+        for dev in (which_axis, dev_axis):
+            row_data = lax.psum(row_data, dev)
+        return row_data
+
+    factor_sum, gram_sum = sites_lead((local_factor, local_gram))
     lower_gram = jnp.linalg.cholesky(gram_sum + ridge_factor * identity)
     factors = jax.scipy.linalg.cho_solve((lower_gram, True), factor_sum.T).T.astype(jnp.bfloat16)
     local_hess = lax.dot_general(factors, factors, contract, preferred_element_type=jnp.float32)

time: 549 us -> 493 us (0.90)
  waiting for transfers between devices: 436 us -> 380 us
    psum x1 -> x2, waiting for transfers between devices: 149 us -> 98.8 us  [sites_lead(): row_data = lax.psum(row_data, dev)]
    psum x1, waiting for transfers between devices: 183 us -> 177 us  [body(): hess_sum, cross_sum = lax.psum((local_hess, local_cross), 'samp')]
  transfers between devices with their start and end apart: 3 -> 4, of which waited for: 3 -> 4; matrix products, arithmetic and copies ran while one was open for 0% -> 0% of each run, Pallas kernels for 0% -> 0%
where the time goes in v1:
time: 493 us
  waiting for transfers between devices  380 us (77%)
  other arithmetic  49.1 us (10%)
  matrix products  24.6 us (5%)
  blocking collectives  21.6 us (4%)
  between operations  13.2 us (3%)
    psum x1, waiting for transfers between devices, body(): hess_sum, cross_sum = lax.psum((local_hess, local_cross), 'samp')  177 us
    all_gather x1, waiting for transfers between devices, body(): lax.all_gather(panel_resid, ('gene', 'snp'), axis=0, tiled=True)  105 us
    psum x2, waiting for transfers between devices, sites_lead(): row_data = lax.psum(row_data, dev)  98.8 us
    all_to_all x1, blocking collectives, body(): lax.all_to_all(residual_t, 'samp', split_axis=0, concat_axis=1, tiled=True)  21.6 us
    dot_general x1, matrix products, body(): jnp.dot(lax.all_gather(panel_resid, ('gene', 'snp'), axis=0, tiled=True),...  14.6 us
    another operation x3, other arithmetic, body(): lower_gram = jnp.linalg.cholesky(gram_sum + ridge_factor * identity)  12.4 us
    another operation x3, other arithmetic, body(): lower_hess = jnp.linalg.cholesky(hess_sum + ridge_sample * identity)  12.4 us
    another operation x2, other arithmetic, body(): jax.scipy.linalg.cho_solve((lower_gram, True), factor_sum.T)  10.5 us
  transfers between devices with their start and end apart: 4, of which 4 were waited for; matrix products, arithmetic and copies ran while one was open for 0% of the time, Pallas kernels for 0%

profile of v1, /device:TPU:1, one launch (start us, length us, event | category | flops | bytes accessed | tf_op | source)
XLA Modules:
  0.0 492.6 jit_solution(10428386252305050897)
XLA Ops:
  6.5 0.9 copy-done
  7.5 0.9 fusion.13
  8.4 2.0 fusion.14
  10.4 50.9 %all-reduce.11.cloned.1.call-done = (f32[256,128]{1,0:T(8,128)}, f32[128,128]{0,1:T(8,128)}) async-done(((f32[256,128]{1,0:T(8,128)}, f32[128,128]{0,1:T(8,128)}), (f32[256,128]{1,0:T(8,128)}, f32[128,128]{0,1:T(8,128)})) %all-reduce.11.cloned.1.call-update) | async-done | bytes 196624 | tf_op jit(solution)/shard_map/psum | solution.py:26
  61.4 47.8 %all-reduce.9.cloned.1.call-done = (f32[256,128]{1,0:T(8,128)}, f32[128,128]{0,1:T(8,128)}) async-done(((f32[256,128]{1,0:T(8,128)}, f32[128,128]{0,1:T(8,128)}), (f32[256,128]{1,0:T(8,128)}, f32[128,128]{0,1:T(8,128)})) %all-reduce.9.cloned.1.call-update) | async-done | bytes 196624 | tf_op jit(solution)/shard_map/psum | solution.py:26
  109.3 0.9 convert_add_fusion.1
  110.2 0.9 fusion.10
  111.1 11.7 %cholesky.44 = f32[128,128]{1,0:T(8,128)S(1)} custom-call(f32[128,128]{1,0:T(8,128)S(1)} %fusion.10), custom_call_target="Cholesky" | custom-call | tf_op jit(solution)/shard_map/jit(cholesky)/cholesky | solution.py:30
  123.5 0.7 fusion.1
  124.1 9.8 %custom-call.16 = f32[1,128,128]{1,2,0:T(8,128)S(1)} custom-call(f32[1,128,128]{2,1,0:T(8,128)S(1)} %fusion.1), custom_call_target="InvertDiagBlocksLowerTriangular" | custom-call | tf_op jit(solution)/shard_map/jit(_cho_solve)/triangular_solve | solution.py:31
  133.9 1.2 fusion.8
  135.6 0.8 fusion.15
  136.4 2.1 fusion.16
  138.7 1.2 copy.17
  140.0 176.9 %all-reduce.7.cloned.1.call-done = (f32[128,1024]{1,0:T(8,128)}, f32[128,128]{0,1:T(8,128)}) async-done(((f32[128,1024]{1,0:T(8,128)}, f32[128,128]{0,1:T(8,128)}), (f32[128,1024]{1,0:T(8,128)}, f32[128,128]{0,1:T(8,128)})) %all-reduce.7.cloned.1.call-update) | async-done | bytes 589840 | tf_op jit(solution)/shard_map/psum | solution.py:34
  316.9 0.9 convert_add_fusion
  317.8 0.9 fusion.6
  318.7 11.7 %cholesky.55 = f32[128,128]{1,0:T(8,128)S(1)} custom-call(f32[128,128]{1,0:T(8,128)S(1)} %fusion.6), custom_call_target="Cholesky" | custom-call | tf_op jit(solution)/shard_map/jit(cholesky)/cholesky | solution.py:35
  331.7 9.8 %custom-call.17 = f32[1,128,128]{1,2,0:T(8,128)S(1)} custom-call(f32[1,128,128]{2,1,0:T(8,128)S(1)} %fusion.2), custom_call_target="InvertDiagBlocksLowerTriangular" | custom-call | tf_op jit(solution)/shard_map/jit(_cho_solve)/triangular_solve | solution.py:36
  341.5 1.7 fusion.4
  344.1 21.6 %all_to_all.19 = bf16[16,64,256]{2,1,0:T(8,128)(2,1)S(1)} all-to-all(bf16[16,64,256]{2,1,0:T(8,128)(2,1)S(1)} %bitcast.48), channel_id=1, replica_groups=mesh['samp'=16,'gene'=4,'snp'=4] {'samp'}, dimensions={0} | all-to-all | bytes 1048576 | tf_op jit(solution)/shard_map/all_to_all | solution.py:41
  365.8 0.8 copy.26
  366.6 104.8 %all-gather.2.cloned.1.call-done = bf16[1024,4096]{1,0:T(8,128)(2,1)} async-done(((bf16[64,4096]{1,0:T(8,128)(2,1)}), bf16[1024,4096]{1,0:T(8,128)(2,1)}) %all-gather.2.cloned.1.call-update) | async-done | bytes 8388624 | tf_op jit(solution)/shard_map/all_gather | solution.py:44
  471.4 14.6 %multiply_convert_fusion = bf16[1024,1024]{1,0:T(8,128)(2,1)} fusion(bf16[1024,4096]{1,0:T(8,128)(2,1)} %all-gather.2.cloned.1.call-done, bf16[4096,1024]{1,0:T(8,128)(2,1)} %param.6), kind=kOutput, calls=%fused_computation | convolution fusion | flops 8592031744 | bytes 18874368 | tf_op jit(solution)/shard_map/dot_general | solution.py:43
  (19 shorter events, 3.9 us)
Async XLA Ops:
  6.5 1.0 copy-start
  6.5 54.8 %all-reduce.11.cloned.1.call-start = ((), (), s32[]{:S(2)}) async-start(), calls=%async_computation.4 | async-start | bytes 393216 | tf_op jit(solution)/shard_map/psum | solution.py:26
  10.4 98.9 %all-reduce.9.cloned.1.call-start = ((), (), s32[]{:S(2)}) async-start(), calls=%async_computation.3 | async-start | bytes 393216 | tf_op jit(solution)/shard_map/psum | solution.py:26
  61.4 255.5 %all-reduce.7.cloned.1.call-start = ((), (), s32[]{:S(2)}) async-start(), calls=%async_computation.2 | async-start | bytes 1179648 | tf_op jit(solution)/shard_map/psum | solution.py:34
  138.5 332.9 %all-gather.2.cloned.1.call-start = ((), (), s32[]{:S(2)}) async-start(), calls=%async_computation.1 | async-start | bytes 8912896 | tf_op jit(solution)/shard_map/all_gather | solution.py:44
Sparse Core Ops, SparseCore 0:
  10.5 50.8 all-reduce.10
  63.8 45.3 all-reduce.8
  138.6 178.1 all-reduce.6
  366.8 104.6 all-gather.1
